TPU v7x, 32 devices: a whole 2x2x4 slice. The times are simulated.
32 devices in a mesh: row: 8 (over y, x, core), col: 4 (over z).
Axes of the slice: x: 2, y: 2, z: 4, core: 2. Of those that a mesh axis runs over, the one named last changes fastest.
Arguments:
- pair_in: bfloat16 [384, 384, 128], P('row', 'col'), may hold values from -6 to 6
- coords: float32 [3, 384], P(None, 'row'), may hold values from -36 to 36
- chain_ids: int32 [384], P('row'), may hold values from 0 to 3, never falling along the last dimension, each value on 1 to 192 neighbouring positions
- coord_mask: int32 [384], P('row'), may hold values 0 or 1
- gain_tri: float32 [128], replicated, may hold values from 0.1 to 1.9
- gain_sum: float32 [128], replicated, may hold values from 0.1 to 1.9
- gain_attn: float32 [128], replicated, may hold values from 0.1 to 1.9
- w_tri_in: bfloat16 [128, 640], replicated, may hold values from -0.5 to 0.5
- w_tri_out: bfloat16 [128, 128], replicated, may hold values from -0.5 to 0.5
- w_bins: float32 [36, 128], replicated, may hold values from -3 to 3
- same_chain: float32 [128], replicated, may hold values from -6 to 6
- w_query: bfloat16 [128, 128], replicated, may hold values from -8 to 8
- w_attn: bfloat16 [128, 384], replicated, may hold values from -0.5 to 0.5
- w_bias: bfloat16 [128, 4], replicated, may hold values from -0.5 to 0.5
- w_attn_out: bfloat16 [128, 128], replicated, may hold values from -0.5 to 0.5
Outputs:
- pair_out: bfloat16 [384, 384, 128], P('row', 'col')
Inputs may be any that keep to these rules, and one draw needn't show every extreme that they name: `chain_ids`: chain numbers never fall along the residues, and no chain holds more than half of them.
All inputs are finite; a program needn't handle non-finite values. No bound on the sum of `coord_mask` on one device may be relied on, other than what follows from the above.
Results may differ from a plain program's by a relative error of at most 0.02.
Values may be sent and summed in bfloat16 or wider, within the bound.
A program may use at most 192 MiB of HBM per device.

v0:
```python
import math
import jax
import jax.numpy as jnp
from jax import lax
from jax.sharding import PartitionSpec as P


def layer_norm(values, gain):
    center = values - jnp.mean(values, axis=-1, keepdims=True)
    spread = jnp.mean(center * center, axis=-1, keepdims=True)
    return center * lax.rsqrt(spread + 1e-05) * gain


def body(
    pair_in,
    coords,
    chain_ids,
    coord_mask,
    gain_tri,
    gain_sum,
    gain_attn,
    w_tri_in,
    w_tri_out,
    w_bins,
    same_chain,
    w_query,
    w_attn,
    w_bias,
    w_attn_out,
):
    row_count, col_count, channels = pair_in.shape
    n_heads = w_bias.shape[1]
    head_size = channels // n_heads
    n_bins = w_bins.shape[0]
    col_start = lax.axis_index("col") * col_count
    coords_all, chains_all, masks_all = (
        lax.all_gather(coords, "row", axis=1, tiled=True),
        lax.all_gather(chain_ids, "row", axis=0, tiled=True),
        lax.all_gather(coord_mask, "row", axis=0, tiled=True),
    )
    pair_wide = pair_in.astype(jnp.float32)
    normed = layer_norm(pair_wide, gain_tri).astype(jnp.bfloat16)
    projected = jnp.dot(
        normed.reshape(row_count * col_count, channels),
        w_tri_in,
        preferred_element_type=jnp.float32,
    ).reshape(row_count, col_count, 5 * channels)
    left_side = (
        (jax.nn.sigmoid(projected[..., :channels]) * projected[..., channels : 2 * channels])
        .astype(jnp.bfloat16)
        .transpose(2, 0, 1)
    )
    right_side = (
        (
            jax.nn.sigmoid(projected[..., 2 * channels : 3 * channels])
            * projected[..., 3 * channels : 4 * channels]
        )
        .astype(jnp.bfloat16)
        .transpose(2, 0, 1)
    )
    tri_gate = jax.nn.sigmoid(projected[..., 4 * channels :])
    right_cols = lax.all_gather(right_side, "row", axis=1, tiled=True)
    summed = lax.psum_scatter(
        jnp.einsum("cjk,cik->jci", right_cols, left_side, preferred_element_type=jnp.float32),
        "col",
        scatter_dimension=0,
        tiled=True,
    )
    product = summed.transpose(2, 0, 1)
    summed_norm = layer_norm(product, gain_sum).astype(jnp.bfloat16)
    pair_one = pair_wide + tri_gate * jnp.dot(
        summed_norm.reshape(row_count * col_count, channels),
        w_tri_out,
        preferred_element_type=jnp.float32,
    ).reshape(row_count, col_count, channels)
    far_coords = lax.dynamic_slice_in_dim(coords_all, col_start, col_count, 1)
    far_chains = lax.dynamic_slice_in_dim(chains_all, col_start, col_count, 0)
    far_masks = lax.dynamic_slice_in_dim(masks_all, col_start, col_count, 0)
    offsets = coords[:, :, None] - far_coords[:, None, :]
    dist = jnp.sqrt(jnp.sum(offsets * offsets, axis=0) + 1.0)
    centres = 2.0 + 20.0 * jnp.arange(n_bins, dtype=jnp.float32) / (n_bins - 1)
    spacing = 25.0 / (n_bins - 1)
    pair_mask = coord_mask.astype(jnp.float32)[:, None] * far_masks.astype(jnp.float32)[None, :]
    feats = jnp.exp(-(((dist[..., None] - centres) / spacing) ** 2)) * pair_mask[..., None]
    binned = jnp.dot(
        feats.reshape(row_count * col_count, n_bins), w_bins, precision=lax.Precision.HIGHEST
    ).reshape(row_count, col_count, channels)
    shared = (chain_ids[:, None] == far_chains[None, :]).astype(jnp.float32)
    pair_two = (pair_one + binned + shared[..., None] * same_chain).astype(jnp.bfloat16)
    normed_two = layer_norm(pair_two.astype(jnp.float32), gain_attn).astype(jnp.bfloat16)
    flat_two = normed_two.reshape(row_count * col_count, channels)
    queries = (
        jnp.dot(flat_two, w_query, preferred_element_type=jnp.float32)
        .astype(jnp.bfloat16)
        .reshape(row_count, col_count, n_heads, head_size)
    )
    gate_pre = jnp.dot(
        flat_two, w_attn[:, 2 * channels :], preferred_element_type=jnp.float32
    ).reshape(row_count, col_count, channels)
    attn_gate = jax.nn.sigmoid(gate_pre)
    pair_bias = (
        jnp.dot(flat_two, w_bias, preferred_element_type=jnp.float32)
        .astype(jnp.bfloat16)
        .reshape(row_count, col_count, n_heads)
        .transpose(2, 0, 1)
    )
    bias_wide = lax.all_gather(pair_bias, "col", axis=2, tiled=True)
    bias_full = lax.all_gather(bias_wide, "row", axis=1, tiled=True)
    bias_mine = lax.dynamic_slice_in_dim(bias_full, col_start, col_count, 1)
    group = math.gcd(row_count, 8)
    blocks = row_count // group
    query_groups = queries.reshape(blocks, group, col_count, n_heads, head_size)
    root_dim = math.sqrt(head_size)
    start_state = (
        jnp.full((blocks, group, n_heads, col_count), -1e30, jnp.float32),
        jnp.zeros((blocks, group, n_heads, col_count), jnp.float32),
        jnp.zeros((blocks, group, n_heads, col_count, head_size), jnp.float32),
    )
    panel = lax.all_gather(normed_two, "col", axis=1, tiled=True)
    span = panel.shape[1]
    both = jnp.dot(
        panel.reshape(row_count * span, channels),
        w_attn[:, : 2 * channels],
        preferred_element_type=jnp.float32,
    ).reshape(row_count, span, 2 * channels)
    key_part = both[..., :channels].astype(jnp.bfloat16)
    span = key_part.shape[1]
    bias_part = bias_mine.astype(jnp.float32)
    key_groups = key_part.reshape(blocks, group, span, n_heads, head_size)
    value_groups = (
        both[..., channels:].astype(jnp.bfloat16).reshape(blocks, group, span, n_heads, head_size)
    )

    def one_block(items):
        query_blk, key_blk, value_blk, running_top, running_total, running_acc = items
        scores = (
            jnp.einsum("ijhd,ikhd->ihjk", query_blk, key_blk, preferred_element_type=jnp.float32)
            / root_dim
            + bias_part[None]
        )
        new_top = jnp.maximum(running_top, jnp.max(scores, axis=-1))
        rescale = jnp.exp(running_top - new_top)
        expo = jnp.exp(scores - new_top[..., None])
        new_total = running_total * rescale + jnp.sum(expo, axis=-1)
        new_acc = running_acc * rescale[..., None] + jnp.einsum(
            "ihjk,ikhd->ihjd",
            expo.astype(jnp.bfloat16),
            value_blk,
            preferred_element_type=jnp.float32,
        )
        return (new_top, new_total, new_acc)

    final_top, final_total, final_acc = lax.map(
        one_block,
        (query_groups, key_groups, value_groups, start_state[0], start_state[1], start_state[2]),
    )
    attended = (
        (final_acc / final_total[..., None])
        .reshape(row_count, n_heads, col_count, head_size)
        .transpose(0, 2, 1, 3)
        .reshape(row_count, col_count, channels)
    )
    gated = (attn_gate * attended).astype(jnp.bfloat16)
    result = pair_two.astype(jnp.float32) + jnp.dot(
        gated.reshape(row_count * col_count, channels),
        w_attn_out,
        preferred_element_type=jnp.float32,
    ).reshape(row_count, col_count, channels)
    return result.astype(jnp.bfloat16)


def solution(mesh):
    return jax.shard_map(
        body,
        mesh=mesh,
        in_specs=(
            P("row", "col", None),
            P(None, "row"),
            P("row"),
            P("row"),
            P(),
            P(),
            P(),
            P(),
            P(),
            P(),
            P(),
            P(),
            P(),
            P(),
            P(),
        ),
        out_specs=P("row", "col", None),
        check_vma=False,
    )
```

profile of v0, /device:TPU:0, one launch (start us, length us, event | category | flops | bytes accessed | tf_op | source)
XLA Modules:
  0.0 504.3 jit_solution(13640466424140914236)
XLA Ops:
  8.4 2.7 fusion.29
  13.2 2.7 fusion.57
  18.9 60.5 %all-gather.5.cloned.1.call-done = bf16[128,384,96]{0,2,1:T(8,128)(2,1)} async-done(((bf16[128,48,96]{0,2,1:T(8,128)(2,1)}), bf16[128,384,96]{0,2,1:T(8,128)(2,1)}) %all-gather.5.cloned.1.call-update) | async-done | bytes 9437200 | tf_op jit(solution)/shard_map/all_gather | solution.py:62
  79.4 15.5 %copy.76 = bf16[128,384,96]{2,1,0:T(8,128)(2,1)} copy(bf16[128,384,96]{0,2,1:T(8,128)(2,1)} %all-gather.5.cloned.1.call-done) | data formatting | bytes 18874368 | tf_op jit(solution)/shard_map/all_gather | solution.py:62
  95.0 13.6 %convolution_bitcast_fusion = f32[384,128,48]{0,2,1:T(8,128)} fusion(bf16[128,48,96]{2,1,0:T(8,128)(2,1)S(1)} %copy.75, bf16[128,384,96]{2,1,0:T(8,128)(2,1)} %copy.76), kind=kOutput, calls=%fused_computation.31 | convolution fusion | flops 452984832 | bytes 20054016 | tf_op jit(solution)/shard_map/cjk,cik->jci/dot_general | solution.py:64
  108.5 9.8 %copy.77 = f32[384,128,48]{1,2,0:T(8,128)} copy(f32[384,128,48]{0,2,1:T(8,128)} %convolution_bitcast_fusion) | data formatting | bytes 18874368 | tf_op jit(solution)/shard_map/cjk,cik->jci/transpose | solution.py:64
  119.0 8.9 %all-gather = f32[8,48,3]{1,2,0:T(4,128)S(1)} all-gather(f32[1,48,3]{1,2,0:T(4,128)S(1)} %bitcast.98), channel_id=1, replica_groups=mesh['row'=8,'col'=4] {'row'}, dimensions={0}, use_global_device_ids=true | all-gather | bytes 5184 | tf_op jit(solution)/shard_map/all_gather | solution.py:37
  129.7 7.0 %all-reduce.2 = (s32[384]{0:T(512)S(1)}, s32[384]{0:T(512)S(1)}) all-reduce(s32[384]{0:T(512)S(1)} %dynamic-update-slice.1, s32[384]{0:T(512)S(1)} %dynamic-update-slice), channel_id=1, replica_groups=mesh['row'=8,'col'=4] {'row'}, use_global_device_ids=true, to_apply=%add.1 | all-reduce | flops 768 | bytes 6144
  137.2 142.5 %reduce-scatter.2.cloned.1.call-done = f32[96,128,48]{1,2,0:T(8,128)} async-done(((f32[384,128,48]{1,2,0:T(8,128)}), f32[96,128,48]{1,2,0:T(8,128)}) %reduce-scatter.2.cloned.1.call-update) | async-done | bytes 2359312 | tf_op jit(solution)/shard_map/reduce_scatter | solution.py:63
  279.7 2.5 bitcast_reduce_fusion
  286.8 7.1 %convert_reduce_fusion = (f32[48,96]{1,0:T(8,128)S(1)}, bf16[48,96,128]{2,1,0:T(8,128)(2,1)S(1)}) fusion(f32[128]{0:T(128)S(1)} %copy-done.20, f32[48,96]{1,0:T(8,128)S(1)} %compare_convert_fusion, f32[36,128]{1,0:T(8,128)S(1)} %copy-done.18, f32[48,96]{1,0:T(8,128)S(1)} %get-tuple-element.114, f32[36]{0:T(128)S(1)} %multiply_add_fusion.1, ...), kind=kOutput, calls=%fused_computation.27 | convolution fusion | flops 262706688 | bytes 7170704 | tf_op jit(solution)/shard_map/dot_general | solution.py:85
  297.8 15.3 %all_gather.26 = bf16[4,48,384]{1,0,2:T(4,128)(2,1)S(1)} all-gather(bf16[4,48,96]{1,0,2:T(4,128)(2,1)S(1)} %bitcast.97), channel_id=1, replica_groups=mesh['row'=8,'col'=4] {'col'}, dimensions={2}, use_global_device_ids=true | all-gather | bytes 184320 | tf_op jit(solution)/shard_map/all_gather | solution.py:107
  318.5 20.2 %all-gather.9.cloned.1.call-done = bf16[4,384,384]{2,0,1:T(4,128)(2,1)} async-done(((bf16[4,48,384]{2,0,1:T(4,128)(2,1)}), bf16[4,384,384]{2,0,1:T(4,128)(2,1)}) %all-gather.9.cloned.1.call-update) | async-done | bytes 1179664 | tf_op jit(solution)/shard_map/all_gather | solution.py:108
  339.8 89.8 %all-gather.7.cloned.1.call-done = bf16[48,384,128]{2,1,0:T(8,128)(2,1)} async-done(((bf16[48,96,128]{2,1,0:T(8,128)(2,1)}), bf16[48,384,128]{2,1,0:T(8,128)(2,1)}) %all-gather.7.cloned.1.call-update) | async-done | bytes 4718608 | tf_op jit(solution)/shard_map/all_gather | solution.py:119
  429.6 8.6 %convolution_convert_fusion = bf16[48,384,256]{1,2,0:T(8,128)(2,1)} fusion(bf16[48,384,128]{2,1,0:T(8,128)(2,1)} %all-gather.7.cloned.1.call-done, bf16[128,384]{1,0:T(8,128)(2,1)} %param.29), kind=kOutput, calls=%fused_computation.22 | convolution fusion | flops 1212678144 | bytes 14221312 | tf_op jit(solution)/shard_map/dot_general | solution.py:121
  438.2 9.3 %fusion.82 = (bf16[48,384,128]{1,2,0:T(8,128)(2,1)}, bf16[48,384,128]{1,2,0:T(8,128)(2,1)}) fusion(bf16[48,384,256]{1,2,0:T(8,128)(2,1)} %convolution_convert_fusion), kind=kLoop, calls=%fused_computation.112 | loop fusion | bytes 18874368 | tf_op jit(solution)/shard_map/slice | solution.py:131
  447.4 41.3 %while.12 = (s32[]{:T(128)}, f32[6,8,4,96]{3,2,1,0:T(4,128)S(1)}, f32[6,8,4,96,32]{3,4,2,1,0:T(8,128)}, bf16[6,8,96,4,32]{2,1,0,4,3:T(8,128)(2,1)S(1)}, bf16[6,8...) while((s32[]{:T(128)}, f32[6,8,4,96]{3,2,1,0:T(4,128)S(1)}, ...), condition=%wide.region_11.12_spmd, body=%wide.region_8.11_spmd.sunk | while | flops 164084736 | bytes 18761308 | solution.py:153
  447.5 2.1 fusion.97
  449.6 3.1 fusion.99
  454.4 2.1 fusion.97
  456.4 3.1 fusion.99
  461.2 2.1 fusion.97
  463.3 3.1 fusion.99
  468.1 2.1 fusion.97
  470.2 3.1 fusion.99
  475.0 2.1 fusion.97
  477.1 3.1 fusion.99
  481.9 2.1 fusion.97
  484.0 3.1 fusion.99
  488.7 2.4 broadcast_divide_fusion
  491.1 2.2 copy.90
  493.3 4.4 fusion.35
  (120 shorter events, 33.9 us)
Async XLA Ops:
  6.5 4.6 copy-start
  6.5 4.6 copy-start.5
  6.5 4.6 copy-start.12
  6.5 72.9 %all-gather.5.cloned.1.call-start = ((), (), s32[]{:S(2)}) async-start(), calls=%async_computation.1 | async-start | bytes 10616832 | tf_op jit(solution)/shard_map/all_gather | solution.py:62
  13.2 4.6 copy-start.2
  17.9 261.8 %reduce-scatter.2.cloned.1.call-start = ((), (), s32[]{:S(2)}) async-start(), calls=%async_computation.2 | async-start | bytes 11796480 | tf_op jit(solution)/shard_map/reduce_scatter | solution.py:63
  118.3 0.7 copy-start.10
  118.3 9.6 %copy-start.19 = (s32[48]{0:T(128)S(1)}, s32[48]{0:T(128)}, u32[]{:S(2)}) copy-start(s32[48]{0:T(128)} %param.20) | copy-start | bytes 580
  118.3 9.6 %copy-start.21 = (u32[32]{0:T(128)S(1)}, u32[32]{0:T(128)}, u32[]{:S(2)}) copy-start(u32[32]{0:T(128)} %constant.69) | copy-start | bytes 388
  118.3 11.1 %copy-start.13 = (s32[48]{0:T(128)S(1)}, s32[48]{0:T(128)}, u32[]{:S(2)}) copy-start(s32[48]{0:T(128)} %param.19) | copy-start | bytes 580
  118.4 220.4 %all-gather.9.cloned.1.call-start = ((), (), s32[]{:S(2)}) async-start(), calls=%async_computation.4 | async-start | bytes 1327104 | tf_op jit(solution)/shard_map/all_gather | solution.py:108
  137.2 146.8 %copy-start.16 = (f32[128]{0:T(128)S(1)}, f32[128]{0:T(128)}, u32[]{:S(2)}) copy-start(f32[128]{0:T(128)} %param.22) | copy-start | bytes 1540
  279.7 2.7 copy-start.3
  283.8 1.7 copy-start.8
  285.5 1.3 copy-start.6
  285.5 1.3 copy-start.18
  285.5 1.3 copy-start.20
  286.8 8.8 %copy-start.14 = (f32[128]{0:T(128)S(1)}, f32[128]{0:T(128)}, u32[]{:S(2)}) copy-start(f32[128]{0:T(128)} %param.23) | copy-start | bytes 1540
  293.9 1.7 copy-start.7
  293.9 3.2 copy-start.11
  297.1 17.2 %copy-start.4 = (bf16[48,96,128]{2,1,0:T(8,128)(2,1)}, bf16[48,96,128]{2,1,0:T(8,128)(2,1)S(1)}, u32[]{:S(2)}) copy-start(bf16[48,96,128]{2,1,0:T(8,128)(2,1)S(1)} %fusion.28) | copy-start | bytes 3538948
  297.1 17.5 %copy-start.9 = (bf16[128,128]{1,0:T(8,128)(2,1)S(1)}, bf16[128,128]{1,0:T(8,128)(2,1)}, u32[]{:S(2)}) copy-start(bf16[128,128]{1,0:T(8,128)(2,1)} %param.28) | copy-start | bytes 98308
  314.0 115.6 %all-gather.7.cloned.1.call-start = ((), (), s32[]{:S(2)}) async-start(), calls=%async_computation.3 | async-start | bytes 5898240 | tf_op jit(solution)/shard_map/all_gather | solution.py:119
  491.1 2.2 copy-start.15
  491.1 2.2 copy-start.17
  493.3 4.4 copy-start.1
Sparse Core Ops, SparseCore 0:
  18.0 61.4 all-gather.4
  118.5 161.1 reduce-scatter.1
  314.1 24.5 all-gather.8
  340.1 89.3 all-gather.6
where the time goes:
time: 506 us; the launch traced here: 504 us
  waiting for transfers between devices  313 us (62%)
  matrix products  69.3 us (14%)
  local copies, waits for them, and re-layouts  46.4 us (9%)
  blocking collectives  31.1 us (6%)
  other arithmetic  29.3 us (6%)
  between operations  14.2 us (3%)
    reduce_scatter x1, waiting for transfers between devices, body(): lax.psum_scatter(jnp.einsum('cjk,cik->jci', right_cols, left_side, prefer...  142 us
    all_gather x1, waiting for transfers between devices, body(): panel = lax.all_gather(normed_two, 'col', axis=1, tiled=True)  89.8 us
    all_gather x1, waiting for transfers between devices, body(): right_cols = lax.all_gather(right_side, 'row', axis=1, tiled=True)  60.5 us
    all_gather x1, waiting for transfers between devices, body(): bias_full = lax.all_gather(bias_wide, 'row', axis=1, tiled=True)  20.2 us
    dot_general x6, matrix products, one_block(): jnp.einsum('ihjk,ikhd->ihjd', expo.astype(jnp.bfloat16), value_blk, prefe...  18.7 us
    all_gather x1, local copies, waits for them, and re-layouts, body(): right_cols = lax.all_gather(right_side, 'row', axis=1, tiled=True)  15.5 us
    all_gather x1, blocking collectives, body(): bias_wide = lax.all_gather(pair_bias, 'col', axis=2, tiled=True)  15.3 us
    dot_general x1, matrix products, body(): jnp.einsum('cjk,cik->jci', right_cols, left_side, preferred_element_type=...  13.6 us
  transfers between devices with their start and end apart: 4, of which 4 were waited for; matrix products, arithmetic and copies ran while one was open for 2% of the time, Pallas kernels for 0%

commit v1 on v0

--- a/solution.py
+++ b/solution.py
@@ -28,6 +28,42 @@
     w_bias,
     w_attn_out,
 ):
+
+    def read_pairs_all_for(x_part, k_dim, base_x, d_out):
+        block_now, block_next, shaped = (
+            lax.axis_size("row"),
+            lax.axis_index("row"),
+            x_part.shape[k_dim],
+        )
+        column = [(i0, (i0 + 1) % block_now) for i0 in range(block_now)]
+        block_list = [(num, j0) for j0, num in column]
+        p_next, v_now = (
+            lax.ppermute(x_part, axis_name="row", perm=column),
+            lax.ppermute(x_part, axis_name="row", perm=block_list),
+        )
+        val = base_x(x_part, block_next * shaped)
+        before = val.shape[d_out]
+        arr_out = jnp.zeros(
+            (*val.shape[:d_out], block_now * before, *val.shape[d_out + 1 :]), val.dtype
+        )
+
+        def _mark_block(arr_out, val, outcome_arr):
+            return lax.dynamic_update_slice_in_dim(arr_out, val, outcome_arr * before, axis=d_out)
+
+        arr_out = _mark_block(arr_out, val, block_next)
+        for j in [*range(1, block_now // 2 + 1)]:
+            work_now, piece_next = ((block_next - j) % block_now, (block_next + j) % block_now)
+            d_next = (p_next, v_now)
+            if j < block_now // 2:
+                p_next, v_now = (
+                    lax.ppermute(p_next, axis_name="row", perm=column),
+                    lax.ppermute(v_now, axis_name="row", perm=block_list),
+                )
+            arr_out = _mark_block(arr_out, base_x(d_next[0], work_now * shaped), work_now)
+            if 2 * j < block_now:
+                arr_out = _mark_block(arr_out, base_x(d_next[1], piece_next * shaped), piece_next)
+        return arr_out
+
     row_count, col_count, channels = pair_in.shape
     n_heads = w_bias.shape[1]
     head_size = channels // n_heads
@@ -59,9 +95,15 @@
         .transpose(2, 0, 1)
     )
     tri_gate = jax.nn.sigmoid(projected[..., 4 * channels :])
-    right_cols = lax.all_gather(right_side, "row", axis=1, tiled=True)
     summed = lax.psum_scatter(
-        jnp.einsum("cjk,cik->jci", right_cols, left_side, preferred_element_type=jnp.float32),
+        read_pairs_all_for(
+            right_side,
+            1,
+            lambda part, at: jnp.einsum(
+                "cjk,cik->jci", part, left_side, preferred_element_type=jnp.float32
+            ),
+            0,
+        ),
         "col",
         scatter_dimension=0,
         tiled=True,

time: 506 us -> 544 us (1.075); the launches traced: 504 us -> 535 us
  waiting for transfers between devices: 313 us -> 273 us
  local copies, waits for them, and re-layouts: 46.4 us -> 85.7 us
  matrix products: 69.3 us -> 88.8 us
  starting transfers between devices: 0.35 us -> 9.43 us
    all_gather x1 -> x0, waiting for transfers between devices: 60.5 us -> none  [body(): right_cols = lax.all_gather(right_side, 'row', axis=1, tiled=True)]
    ppermute x0 -> x7, waiting for transfers between devices: none -> 19.5 us  [the longest x1 19.5 us: read_pairs_all_for(): lax.ppermute(x_part, axis_name='row', perm=column)]
    ppermute x0 -> x7, local copies, waits for them, and re-layouts: none -> 19.5 us  [the longest x3 8.34 us: read_pairs_all_for(): lax.ppermute(p_next, axis_name='row', perm=column)]
    dot_general x1 -> x8, matrix products: 13.6 us -> 32 us  [body(): jnp.einsum('cjk,cik->jci', part, left_side, preferred_element_type=jnp.fl...]
    transpose x1 -> x9, local copies, waits for them, and re-layouts: 9.79 us -> 27.5 us  [the longest x8 24.8 us: body(): jnp.einsum('cjk,cik->jci', part, left_side, preferred_element_type=jnp.fl...]
    all_gather x1 -> x0, local copies, waits for them, and re-layouts: 15.5 us -> none  [body(): right_cols = lax.all_gather(right_side, 'row', axis=1, tiled=True)]
    dynamic_update_slice x0 -> x8, local copies, waits for them, and re-layouts: none -> 13.1 us  [_mark_block(): lax.dynamic_update_slice_in_dim(arr_out, val, outcome_arr * before, axis=...]
    ppermute x0 -> x7, starting transfers between devices: none -> 9.13 us  [the longest x2 4.73 us: read_pairs_all_for(): lax.ppermute(v_now, axis_name='row', perm=block_list)]
  transfers between devices with their start and end apart: 4 -> 10, of which waited for: 4 -> 4; matrix products, arithmetic and copies ran while one was open for 2% -> 18% of each run, Pallas kernels for 0% -> 0%
where the time goes in v1:
time: 544 us; the launch traced here: 535 us
  waiting for transfers between devices  273 us (50%)
  matrix products  88.8 us (16%)
  local copies, waits for them, and re-layouts  85.7 us (16%)
  blocking collectives  34.2 us (6%)
  other arithmetic  28.7 us (5%)
  between operations  14.5 us (3%)
  starting transfers between devices  9.43 us (2%)
    reduce_scatter x1, waiting for transfers between devices, body(): lax.psum_scatter(read_pairs_all_for(right_side, 1, lambda part, at: jnp.e...  143 us
    all_gather x1, waiting for transfers between devices, body(): panel = lax.all_gather(normed_two, 'col', axis=1, tiled=True)  89.9 us
    dot_general x8, matrix products, body(): jnp.einsum('cjk,cik->jci', part, left_side, preferred_element_type=jnp.fl...  32 us
    transpose x8, local copies, waits for them, and re-layouts, body(): jnp.einsum('cjk,cik->jci', part, left_side, preferred_element_type=jnp.fl...  24.8 us
    all_gather x1, waiting for transfers between devices, body(): bias_full = lax.all_gather(bias_wide, 'row', axis=1, tiled=True)  20 us
    ppermute x1, waiting for transfers between devices, read_pairs_all_for(): lax.ppermute(x_part, axis_name='row', perm=column)  19.5 us
    dot_general x6, matrix products, one_block(): jnp.einsum('ihjk,ikhd->ihjd', expo.astype(jnp.bfloat16), value_blk, prefe...  18.8 us
    all_gather x1, blocking collectives, body(): bias_wide = lax.all_gather(pair_bias, 'col', axis=2, tiled=True)  15.3 us
  transfers between devices with their start and end apart: 10, of which 4 were waited for; matrix products, arithmetic and copies ran while one was open for 18% of the time, Pallas kernels for 0%

profile of v1, /device:TPU:0, one launch (start us, length us, event | category | flops | bytes accessed | tf_op | source)
XLA Modules:
  0.0 534.9 jit_solution(11310360852232249790)
XLA Ops:
  26.4 19.5 %collective-permute-done = bf16[128,48,96]{0,2,1:T(8,128)(2,1)} collective-permute-done((bf16[128,48,96]{0,2,1:T(8,128)(2,1)}, bf16[128,48,96]{0,2,1:T(8,128)(2,1)}, u32[]{:S(2)}, u32[]{:S(2)}) %collective-permute-start) | collective-permute-done | bytes 1179680 | tf_op jit(solution)/shard_map/ppermute | solution.py:41
  46.5 4.0 convolution_bitcast_fusion.7
  50.5 3.2 copy.137
  55.7 4.7 broadcast_in_dim.6
  64.3 4.0 convolution_bitcast_fusion.6
  68.3 3.2 copy.140
  74.3 4.0 convolution_bitcast_fusion.5
  78.3 3.2 copy.143
  91.0 4.0 convolution_bitcast_fusion.4
  95.0 3.2 copy.146
  100.9 4.0 convolution_bitcast_fusion.3
  104.9 3.2 copy.149
  114.6 4.0 convolution_bitcast_fusion.2
  118.6 3.2 copy.152
  124.5 4.0 convolution_bitcast_fusion.1
  128.5 3.2 copy.155
  138.2 4.0 convolution_bitcast_fusion
  146.4 11.4 %all-gather = f32[8,48,3]{1,2,0:T(4,128)S(1)} all-gather(f32[1,48,3]{1,2,0:T(4,128)S(1)} %bitcast.127), channel_id=1, replica_groups=mesh['row'=8,'col'=4] {'row'}, dimensions={0}, use_global_device_ids=true | all-gather | bytes 5184 | tf_op jit(solution)/shard_map/all_gather | solution.py:73
  159.7 7.6 %all-reduce.2 = (s32[384]{0:T(512)S(1)}, s32[384]{0:T(512)S(1)}) all-reduce(s32[384]{0:T(512)S(1)} %dynamic-update-slice.1, s32[384]{0:T(512)S(1)} %dynamic-update-slice), channel_id=1, replica_groups=mesh['row'=8,'col'=4] {'row'}, use_global_device_ids=true, to_apply=%add.1 | all-reduce | flops 768 | bytes 6144
  167.7 143.4 %reduce-scatter.2.cloned.1.call-done = f32[96,128,48]{1,0,2:T(8,128)} async-done(((f32[384,128,48]{1,0,2:T(8,128)}), f32[96,128,48]{1,0,2:T(8,128)}) %reduce-scatter.2.cloned.1.call-update) | async-done | bytes 2359312 | tf_op jit(solution)/shard_map/reduce_scatter | solution.py:98
  317.0 7.0 %convert_reduce_fusion = (f32[48,96]{1,0:T(8,128)S(1)}, bf16[48,96,128]{2,1,0:T(8,128)(2,1)S(1)}) fusion(f32[128]{0:T(128)S(1)} %copy-done.23, f32[48,96]{1,0:T(8,128)S(1)} %compare_convert_fusion, f32[36,128]{1,0:T(8,128)S(1)} %copy-done.21, f32[48,96]{1,0:T(8,128)S(1)} %get-tuple-element.107, f32[36]{0:T(128)S(1)} %multiply_add_fusion.1, ...), kind=kOutput, calls=%fused_computation.27 | convolution fusion | flops 262706688 | bytes 7170704 | tf_op jit(solution)/shard_map/dot_general | solution.py:127
  328.0 15.3 %all_gather.22 = bf16[4,48,384]{1,0,2:T(4,128)(2,1)S(1)} all-gather(bf16[4,48,96]{1,0,2:T(4,128)(2,1)S(1)} %bitcast.126), channel_id=1, replica_groups=mesh['row'=8,'col'=4] {'col'}, dimensions={2}, use_global_device_ids=true | all-gather | bytes 184320 | tf_op jit(solution)/shard_map/all_gather | solution.py:149
  348.8 20.0 %all-gather.6.cloned.1.call-done = bf16[4,384,384]{2,0,1:T(4,128)(2,1)} async-done(((bf16[4,48,384]{2,0,1:T(4,128)(2,1)}), bf16[4,384,384]{2,0,1:T(4,128)(2,1)}) %all-gather.6.cloned.1.call-update) | async-done | bytes 1179664 | tf_op jit(solution)/shard_map/all_gather | solution.py:150
  370.0 89.9 %all-gather.4.cloned.1.call-done = bf16[48,384,128]{2,1,0:T(8,128)(2,1)} async-done(((bf16[48,96,128]{2,1,0:T(8,128)(2,1)}), bf16[48,384,128]{2,1,0:T(8,128)(2,1)}) %all-gather.4.cloned.1.call-update) | async-done | bytes 4718608 | tf_op jit(solution)/shard_map/all_gather | solution.py:161
  459.9 8.6 %convolution_convert_fusion = bf16[48,384,256]{1,2,0:T(8,128)(2,1)} fusion(bf16[48,384,128]{2,1,0:T(8,128)(2,1)} %all-gather.4.cloned.1.call-done, bf16[128,384]{1,0:T(8,128)(2,1)} %param.29), kind=kOutput, calls=%fused_computation.22 | convolution fusion | flops 1212678144 | bytes 14221312 | tf_op jit(solution)/shard_map/dot_general | solution.py:163
  468.5 9.2 %fusion.85 = (bf16[48,384,128]{1,2,0:T(8,128)(2,1)}, bf16[48,384,128]{1,2,0:T(8,128)(2,1)}) fusion(bf16[48,384,256]{1,2,0:T(8,128)(2,1)} %convolution_convert_fusion), kind=kLoop, calls=%fused_computation.130 | loop fusion | bytes 18874368 | tf_op jit(solution)/shard_map/slice | solution.py:173
  477.7 41.3 %while.12 = (s32[]{:T(128)}, f32[6,8,4,96]{3,2,1,0:T(4,128)S(1)}, f32[6,8,4,96,32]{3,4,2,1,0:T(8,128)}, bf16[6,8,96,4,32]{2,1,0,4,3:T(8,128)(2,1)S(1)}, bf16[6,8...) while((s32[]{:T(128)}, f32[6,8,4,96]{3,2,1,0:T(4,128)S(1)}, ...), condition=%wide.region_11.12_spmd, body=%wide.region_8.11_spmd.sunk | while | flops 164084736 | bytes 18761308 | solution.py:195
  479.9 3.1 fusion.116
  486.8 3.1 fusion.116
  500.5 3.1 fusion.116
  514.3 3.1 fusion.116
  523.7 4.5 fusion.35
  (162 shorter events, 112.1 us)
Async XLA Ops:
  6.5 4.6 copy-start
  6.5 4.6 copy-start.5
  6.5 4.6 copy-start.15
  6.5 304.6 %reduce-scatter.2.cloned.1.call-start = ((), (), s32[]{:S(2)}) async-start(), calls=%async_computation.1 | async-start | bytes 11796480 | tf_op jit(solution)/shard_map/reduce_scatter | solution.py:98
  13.2 5.0 copy-start.2
  18.3 27.6 %collective-permute-start = (bf16[128,48,96]{0,2,1:T(8,128)(2,1)}, bf16[128,48,96]{0,2,1:T(8,128)(2,1)}, u32[]{:S(2)}, u32[]{:S(2)}) collective-permute-start(bf16[128,48,96]{0,2,1:T(8,128)(2,1)} %get-tuple-element.100), channel_id=1, source_target_pairs={{0,4},{4,8},{8,12},{12,16},{16,20},{20,24},{24,28},{28,0},{1,5},{5... | collective-permute-start | bytes 3538952 | tf_op jit(solution)/shard_map/ppermute | solution.py:41
  18.8 34.9 %collective-permute-start.1 = (bf16[128,48,96]{0,2,1:T(8,128)(2,1)}, bf16[128,48,96]{0,2,1:T(8,128)(2,1)}, u32[]{:S(2)}, u32[]{:S(2)}) collective-permute-start(bf16[128,48,96]{0,2,1:T(8,128)(2,1)} %get-tuple-element.100), channel_id=1, source_target_pairs={{4,0},{8,4},{12,8},{16,12},{20,16},{24,20},{28,24},{0,28},{5,1},{9... | collective-permute-start | bytes 3538952 | tf_op jit(solution)/shard_map/ppermute | solution.py:42
  45.9 35.6 %collective-permute-start.2 = (bf16[128,48,96]{0,2,1:T(8,128)(2,1)}, bf16[128,48,96]{0,2,1:T(8,128)(2,1)}, u32[]{:S(2)}, u32[]{:S(2)}) collective-permute-start(bf16[128,48,96]{0,2,1:T(8,128)(2,1)} %collective-permute-done), channel_id=1, source_target_pairs={{0,4},{4,8},{8,12},{12,16},{16,20},{20,24},{24,28},{28,0},{1,5},{5... | collective-permute-start | bytes 3538952 | tf_op jit(solution)/shard_map/ppermute | solution.py:59
  53.7 6.7 %copy-start.6 = (f32[48,128,48]{1,0,2:T(8,128)S(1)}, f32[48,128,48]{1,0,2:T(8,128)}, u32[]{:S(2)}) copy-start(f32[48,128,48]{1,0,2:T(8,128)} %copy.137) | copy-start | bytes 3538948
  53.7 34.6 %collective-permute-start.3 = (bf16[128,48,96]{0,2,1:T(8,128)(2,1)}, bf16[128,48,96]{0,2,1:T(8,128)(2,1)}, u32[]{:S(2)}, u32[]{:S(2)}) collective-permute-start(bf16[128,48,96]{0,2,1:T(8,128)(2,1)} %collective-permute-done.1), channel_id=1, source_target_pairs={{4,0},{8,4},{12,8},{16,12},{20,16},{24,20},{28,24},{0,28},{5,1},{9... | collective-permute-start | bytes 3538952 | tf_op jit(solution)/shard_map/ppermute | solution.py:60
  81.5 2.9 copy-start.8
  81.5 29.2 %collective-permute-start.4 = (bf16[128,48,96]{0,2,1:T(8,128)(2,1)}, bf16[128,48,96]{0,2,1:T(8,128)(2,1)}, u32[]{:S(2)}, u32[]{:S(2)}) collective-permute-start(bf16[128,48,96]{0,2,1:T(8,128)(2,1)} %collective-permute-done.2), channel_id=1, source_target_pairs={{0,4},{4,8},{8,12},{12,16},{16,20},{20,24},{24,28},{28,0},{1,5},{5... | collective-permute-start | bytes 3538952 | tf_op jit(solution)/shard_map/ppermute | solution.py:59
  88.3 33.5 %collective-permute-start.5 = (bf16[128,48,96]{0,2,1:T(8,128)(2,1)}, bf16[128,48,96]{0,2,1:T(8,128)(2,1)}, u32[]{:S(2)}, u32[]{:S(2)}) collective-permute-start(bf16[128,48,96]{0,2,1:T(8,128)(2,1)} %collective-permute-done.3), channel_id=1, source_target_pairs={{4,0},{8,4},{12,8},{16,12},{20,16},{24,20},{28,24},{0,28},{5,1},{9... | collective-permute-start | bytes 3538952 | tf_op jit(solution)/shard_map/ppermute | solution.py:60
  108.2 2.5 copy-start.9
  110.7 24.7 %collective-permute-start.6 = (bf16[128,48,96]{0,2,1:T(8,128)(2,1)}, bf16[128,48,96]{0,2,1:T(8,128)(2,1)}, u32[]{:S(2)}, u32[]{:S(2)}) collective-permute-start(bf16[128,48,96]{0,2,1:T(8,128)(2,1)} %collective-permute-done.4), channel_id=1, source_target_pairs={{0,4},{4,8},{8,12},{12,16},{16,20},{20,24},{24,28},{28,0},{1,5},{5... | collective-permute-start | bytes 3538952 | tf_op jit(solution)/shard_map/ppermute | solution.py:59
  131.8 2.5 copy-start.10
  145.7 12.2 %copy-start.22 = (s32[48]{0:T(128)S(1)}, s32[48]{0:T(128)}, u32[]{:S(2)}) copy-start(s32[48]{0:T(128)} %param.20) | copy-start | bytes 580
  145.7 12.2 %copy-start.24 = (u32[32]{0:T(128)S(1)}, u32[32]{0:T(128)}, u32[]{:S(2)}) copy-start(u32[32]{0:T(128)} %constant.128) | copy-start | bytes 388
  145.7 13.7 %copy-start.17 = (s32[48]{0:T(128)S(1)}, s32[48]{0:T(128)}, u32[]{:S(2)}) copy-start(s32[48]{0:T(128)} %param.19) | copy-start | bytes 580
  145.8 223.1 %all-gather.6.cloned.1.call-start = ((), (), s32[]{:S(2)}) async-start(), calls=%async_computation.3 | async-start | bytes 1327104 | tf_op jit(solution)/shard_map/all_gather | solution.py:150
  167.7 147.9 %copy-start.11 = (bf16[128,128]{1,0:T(8,128)(2,1)S(1)}, bf16[128,128]{1,0:T(8,128)(2,1)}, u32[]{:S(2)}) copy-start(bf16[128,128]{1,0:T(8,128)(2,1)} %param.25) | copy-start | bytes 98308
  167.7 147.9 %copy-start.16 = (f32[128]{0:T(128)S(1)}, f32[128]{0:T(128)}, u32[]{:S(2)}) copy-start(f32[128]{0:T(128)} %param.22) | copy-start | bytes 1540
  311.1 2.7 copy-start.3
  317.0 8.8 %copy-start.18 = (f32[128]{0:T(128)S(1)}, f32[128]{0:T(128)}, u32[]{:S(2)}) copy-start(f32[128]{0:T(128)} %param.23) | copy-start | bytes 1540
  324.1 1.7 copy-start.7
  324.1 3.2 copy-start.14
  327.3 17.2 %copy-start.4 = (bf16[48,96,128]{2,1,0:T(8,128)(2,1)}, bf16[48,96,128]{2,1,0:T(8,128)(2,1)S(1)}, u32[]{:S(2)}) copy-start(bf16[48,96,128]{2,1,0:T(8,128)(2,1)S(1)} %fusion.28) | copy-start | bytes 3538948
  327.3 17.6 %copy-start.12 = (bf16[128,128]{1,0:T(8,128)(2,1)S(1)}, bf16[128,128]{1,0:T(8,128)(2,1)}, u32[]{:S(2)}) copy-start(bf16[128,128]{1,0:T(8,128)(2,1)} %param.28) | copy-start | bytes 98308
  344.2 115.7 %all-gather.4.cloned.1.call-start = ((), (), s32[]{:S(2)}) async-start(), calls=%async_computation.2 | async-start | bytes 5898240 | tf_op jit(solution)/shard_map/all_gather | solution.py:161
  521.4 2.2 copy-start.19
  521.4 2.2 copy-start.20
  523.7 4.5 copy-start.1
  (3 other events, 3.6 us)
Sparse Core Ops, SparseCore 0:
  145.9 165.2 reduce-scatter.1
  344.3 24.5 all-gather.5
  370.4 89.3 all-gather.3
